TPU v7x, 32 devices: a whole 2x2x4 slice. The times are simulated.
32 devices in a mesh: chain: 2 (over y), px: 8 (over z, x), py: 2 (over core).
Axes of the slice: x: 2, y: 2, z: 4, core: 2. Of those that a mesh axis runs over, the one named last changes fastest.
Arguments:
- adjoint: float32 [512, 256, 256], P(('chain', 'px'), 'py'), parts along dimension 0, may hold values from -6 to 6
- saved: float32 [512, 256, 256], P(('chain', 'px'), 'py'), parts along dimension 0, may hold values from -6 to 6
- spectra: bfloat16 [2, 256, 256, 256], P(None, None, 'px'), may hold values from -6 to 6, as said below
- freq_index: int32 [8], replicated, may hold values from 1 to 8
- picked: int32 [2], replicated, may hold values from 0 to 7
Outputs:
- force: float32 [512, 256, 256], P(('chain', 'px'), 'py'), parts along dimension 0
There are 2 independent parts, one for each index of `chain`. A program takes and returns all parts, laid end to end along the dimension named above; an argument that names none is the same for every part. Nothing has to cross between parts.
Inputs may be any that keep to these rules, and one draw needn't show every extreme that they name: Each kernel is even in every momentum coordinate separately: spectra[j][k1, k2, k3] is unchanged when k1 is replaced by (256 - k1) mod 256, and likewise k2 with 256 and k3 with 256.
All inputs are finite; a program needn't handle non-finite values.
Results may differ from a plain program's by a relative error of at most 0.0003.
Values sent between devices are 32-bit elements; how exact they have to be, the bound alone decides.
A program may use at most 128 MiB of HBM per device.

v0:
```python
import functools
import math

import jax
import jax.numpy as jnp
import numpy as np
from jax import lax
from jax.experimental import pallas as pl
from jax.experimental.pallas import tpu as pltpu
from jax.sharding import PartitionSpec as P


def hartley(length):
    counter = np.arange(length, dtype=np.int64)
    angle = (counter[:, None] * counter[None, :] % length) * (2.0 * np.pi / length)
    return np.cos(angle) + np.sin(angle)


def chosen_index(freq_index, picked):
    ids = jnp.arange(freq_index.shape[0], dtype=jnp.int32)
    return jnp.sum(jnp.where(ids[None, :] == picked[:, None], freq_index[None, :], 0), axis=1)


def along(equation, field, table):
    return jnp.einsum(equation, field, jnp.asarray(table, jnp.float32), precision=lax.Precision.HIGH)


def plain_path(adjoint, saved, spectra, chosen):
    size_px, size_py = lax.axis_size("px"), lax.axis_size("py")
    one, two, three = adjoint.shape[0] * size_px, adjoint.shape[1] * size_py, adjoint.shape[2]
    t_one, t_two, t_three = hartley(one), hartley(two), hartley(three)
    width = three // size_py
    field = along("abc,cz->abz", adjoint, t_three)
    field = lax.all_to_all(field, "py", split_axis=2, concat_axis=1, tiled=True)
    field = along("abc,bz->azc", field, t_two)
    field = lax.all_to_all(field, "px", split_axis=1, concat_axis=0, tiled=True)
    spectrum = along("abc,az->zbc", field, t_one)
    kernels = lax.dynamic_slice_in_dim(spectra, lax.axis_index("py") * width, width, 3)
    omegas = chosen.astype(jnp.float32) * (math.pi / 8.0)
    scale = 1.0 / (one * two * three)
    total = jnp.zeros(saved.shape, jnp.float32)
    for slot in range(chosen.shape[0]):
        back = along("abc,az->zbc", spectrum * kernels[slot].astype(jnp.float32), t_one)
        back = lax.all_to_all(back, "px", split_axis=0, concat_axis=1, tiled=True)
        back = along("abc,bz->azc", back, t_two)
        back = lax.all_to_all(back, "py", split_axis=1, concat_axis=2, tiled=True)
        back = along("abc,cz->abz", back, t_three) * scale
        total = total + omegas[slot] * jnp.cos(omegas[slot] * saved) * back
    return total


def as_three(matrix, axis):
    high = matrix.astype(jnp.bfloat16)
    low = (matrix - high.astype(np.float64)).astype(jnp.bfloat16)
    order = (high, high, low)
    return jnp.asarray(np.concatenate(order, axis=axis))


def split(value, axis):
    high = value.astype(jnp.bfloat16)
    low = (value - high.astype(jnp.float32)).astype(jnp.bfloat16)
    return jnp.concatenate([high, low, high], axis=axis)


def from_right(rows, table):
    return jnp.dot(split(rows, 1), table, preferred_element_type=jnp.float32)


def from_left(table, columns):
    return jnp.dot(table, split(columns, 0), preferred_element_type=jnp.float32)


def params(**more):
    return pltpu.CompilerParams(vmem_limit_bytes=58 << 20, **more)


def core_exchange(step, steps, source, target, sems):
    send_sem, recv_sem, own_sem = sems
    me = lax.axis_index("py")
    other = 1 - me

    def away(at, sender, receiver):
        return pltpu.make_async_remote_copy(
            src_ref=source(receiver, at),
            dst_ref=target(sender, at),
            send_sem=send_sem.at[at],
            recv_sem=recv_sem.at[at],
            device_id={"py": receiver},
            device_id_type=pl.DeviceIdType.MESH,
        )

    def stay(at):
        return pltpu.make_async_copy(source(me, at), target(me, at), own_sem.at[at])

    away(step, me, other).start()
    stay(step).start()

    @pl.when(step == steps - 1)
    def _():
        @pl.loop(0, steps)
        def _(at):
            away(at, me, other).wait_send()
            away(at, other, me).wait_recv()
            stay(at).wait()


def greet_core():
    barrier = pltpu.get_barrier_semaphore()
    other = 1 - lax.axis_index("py")
    pl.semaphore_signal(
        barrier, inc=1, device_id={"py": other}, device_id_type=pl.DeviceIdType.MESH
    )
    pl.semaphore_wait(barrier, 1)


def third_kernel(steps, field_ref, table_ref, out_ref, mine, *sems):
    planes, lines, three = field_ref.shape
    parts, width = mine.shape[0], mine.shape[3]
    step = pl.program_id(0)
    pl.when(step == 0)(greet_core)

    def rows(at):
        return pl.ds(pl.multiple_of(at * planes, planes), planes)

    result = from_right(field_ref[...].reshape(planes * lines, three), table_ref[...])
    for part in range(parts):
        piece = result[:, part * width : (part + 1) * width]
        mine[part, rows(step)] = piece.reshape(planes, lines, width)
    core_exchange(
        step,
        steps,
        lambda part, at: mine.at[part, rows(at)],
        lambda part, at: out_ref.at[part, rows(at)],
        sems,
    )


def second_kernel(field_ref, table_ref, out_ref, held):
    parts, planes, _, width = field_ref.shape
    size_px, local, _, _ = out_ref.shape
    for plane in range(0, planes, 2):
        sides = [
            jnp.concatenate([field_ref[part, at] for part in range(parts)], axis=0)
            for at in (plane, plane + 1)
        ]
        result = from_left(table_ref[...], jnp.concatenate(sides, axis=1))
        held[plane] = result[:, :width]
        held[plane + 1] = result[:, width:]
    for peer in range(size_px):
        out_ref[peer] = jnp.swapaxes(held[:, peer * local : (peer + 1) * local, :], 0, 1)


def second_back_kernel(steps, field_ref, table_ref, out_ref, held, mine, *sems):
    _, groups, local, planes, width = field_ref.shape
    parts, lines = mine.shape[0], mine.shape[3]
    inner = steps // mine.shape[1]
    step = pl.program_id(0) * inner + pl.program_id(1)
    slot = pl.program_id(0)
    begin = pl.program_id(1) * planes
    pl.when(step == 0)(greet_core)
    for group in range(groups):
        held[:, group * local : (group + 1) * local, :] = jnp.swapaxes(field_ref[0, group], 0, 1)
    for plane in range(0, planes, 2):
        columns = jnp.concatenate([held[plane], held[plane + 1]], axis=1)
        result = from_left(table_ref[...], columns)
        for part in range(parts):
            rows = result[part * lines : (part + 1) * lines]
            mine[part, slot, begin + plane] = rows[:, :width]
            mine[part, slot, begin + plane + 1] = rows[:, width:]

    def block(ref):
        return lambda part, at: ref.at[part, at // inner, pl.ds((at % inner) * planes, planes)]

    core_exchange(step, steps, block(mine), block(out_ref), sems)


def cosine_turns(turns):
    turns = turns - jnp.floor(turns + 0.5)
    square = turns * turns * (4.0 * math.pi * math.pi)
    value = jnp.full_like(square, 1.0 / math.factorial(20))
    for order in range(9, -1, -1):
        value = value * square + (-1.0) ** order / math.factorial(2 * order)
    return value


def third_back_kernel(scale, chosen_ref, field_ref, saved_ref, table_ref, out_ref):
    parts, slots, planes, lines, width = field_ref.shape
    three = parts * width
    total = None
    site = saved_ref[...].reshape(planes * lines, three)
    for slot in range(slots):
        sides = [field_ref[part, slot].reshape(planes * lines, width) for part in range(parts)]
        field = from_right(jnp.concatenate(sides, axis=1), table_ref[...])
        index = chosen_ref[slot].astype(jnp.float32)
        weight = cosine_turns(site * (index * (1.0 / 16.0))) * (index * (math.pi / 8.0 * scale))
        total = weight * field if total is None else total + weight * field
    out_ref[...] = total.reshape(planes, lines, three)


def middle_kernel(
    chunks,
    field_ref,
    spectra_ref,
    table_ref,
    out_ref,
    gathered,
    raw,
    kernels,
    product,
    go_send,
    go_recv,
    back_send,
    back_recv,
    plane_send,
    plane_recv,
    own_sem,
    back_own,
    raw_sem,
):
    half, rows_all, planes, width = field_ref.shape
    size_px, local = 2 * half, rows_all // 2
    slots, one = raw.shape[0], raw.shape[1]
    step = local // chunks
    me = lax.axis_index("px")
    part = lax.axis_index("py")
    lower = me < half
    base = jnp.where(lower, 0, half)
    place = me - base

    def block_of(owner):
        return jnp.where(owner < half, owner, size_px - 1 - owner)

    def other(turn):
        return half - base + lax.rem(place + turn, half)

    def mate(turn):
        return base + lax.rem(place + turn, half)

    def to(index):
        return dict(device_id={"px": index}, device_id_type=pl.DeviceIdType.MESH)

    def go(chunk, sender, receiver):
        rows = pl.ds(chunk * 2 * step, 2 * step)
        return pltpu.make_async_remote_copy(
            src_ref=field_ref.at[block_of(receiver), rows],
            dst_ref=gathered.at[sender, rows],
            send_sem=go_send.at[chunk, receiver],
            recv_sem=go_recv.at[chunk, sender],
            **to(receiver),
        )

    def back(slot, chunk, sender, receiver):
        rows = pl.ds(chunk * 2 * step, 2 * step)
        return pltpu.make_async_remote_copy(
            src_ref=product.at[slot, receiver - base, rows],
            dst_ref=out_ref.at[slot, block_of(sender), rows],
            send_sem=back_send.at[slot, chunk, receiver - base],
            recv_sem=back_recv.at[slot, chunk, sender - base],
            **to(receiver),
        )

    def plane(kind, send, receiver):
        return pltpu.make_async_remote_copy(
            src_ref=kernels.at[:, 0],
            dst_ref=kernels.at[:, local + kind],
            send_sem=plane_send.at[send],
            recv_sem=plane_recv.at[kind],
            **to(receiver),
        )

    own = pltpu.make_async_copy(field_ref.at[block_of(me)], gathered.at[me], own_sem)
    fetch = pltpu.make_async_copy(spectra_ref.at[:, :, :, pl.ds(part * width, width)], raw, raw_sem)
    own.start()
    fetch.start()

    barrier = pltpu.get_barrier_semaphore()

    @pl.loop(1, size_px)
    def _(turn):
        pl.semaphore_signal(barrier, inc=1, **to(lax.rem(me + turn, size_px)))

    pl.semaphore_wait(barrier, size_px - 1)

    def send_chunk(at):
        chunk = chunks - 1 - at

        @pl.loop(0, half)
        def _(turn):
            go(chunk, me, other(turn)).start()

        @pl.loop(1, half)
        def _(turn):
            go(chunk, me, mate(turn)).start()

    early = chunks // 2
    pl.loop(0, early)(send_chunk)
    own.wait()
    fetch.wait()
    block = 16

    @pl.loop(0, one // block)
    def _(at):
        rows = pl.ds(pl.multiple_of(at * block, block), block)
        for slot in range(slots):
            piece = raw[slot, rows].astype(jnp.float32)
            kernels[slot, 0:local, rows, :] = jnp.swapaxes(piece, 0, 1)

    before = lax.rem(me + size_px - 1, size_px)
    ends = (me == 0) | (me == size_px - 1)

    @pl.when(before >= half)
    def _():
        plane(0, 0, before).start()

    @pl.when(me == half)
    def _():
        plane(1, 1, 0).start()
        plane(1, 2, size_px - 1).start()

    pl.loop(early, chunks)(send_chunk)

    @pl.loop(0, chunks)
    def _(at):
        chunk = chunks - 1 - at

        @pl.loop(0, half)
        def _(turn):
            go(chunk, other(turn), me).wait_recv()

        @pl.loop(1, half)
        def _(turn):
            go(chunk, mate(turn), me).wait_recv()

        @pl.when(chunk == 0)
        def _():
            @pl.when(jnp.logical_not(lower))
            def _():
                plane(0, 0, before).wait_recv()

            @pl.when(ends)
            def _():
                plane(1, 1, before).wait_recv()

        own_sites = pl.ds(pl.multiple_of(base * planes, half * planes), half * planes)

        @pl.loop(0, step)
        def _(inner):
            line = chunk * step + inner
            first, second = 2 * line, 2 * line + 1
            columns = jnp.concatenate(
                [gathered[:, at].reshape(one, width) for at in (first, second)], axis=1
            )
            spectrum = from_left(table_ref[...], columns)
            leading = line == 0
            plain = jnp.where(lower, line, local - line)
            mirrored = jnp.where(leading & ends, local + 1, plain)
            for slot in range(slots):
                factor = jnp.concatenate([kernels[slot, plain], kernels[slot, mirrored]], axis=1)
                result = from_left(table_ref[own_sites, :], spectrum * factor)
                product[slot, :, first] = result[:, :width].reshape(half, planes, width)
                product[slot, :, second] = result[:, width:].reshape(half, planes, width)

        for slot in range(slots):

            @pl.loop(1, half)
            def _(turn):
                back(slot, chunk, me, mate(turn)).start()

    homes = [
        pltpu.make_async_copy(
            product.at[slot, place], out_ref.at[slot, block_of(me)], back_own.at[slot]
        )
        for slot in range(slots)
    ]
    for home in homes:
        home.start()

    @pl.loop(0, chunks)
    def _(chunk):
        @pl.loop(1, size_px)
        def _(turn):
            go(chunk, me, lax.rem(me + turn, size_px)).wait_send()

        @pl.loop(1, half)
        def _(turn):
            for slot in range(slots):
                back(slot, chunk, me, mate(turn)).wait_send()
                back(slot, chunk, mate(turn), me).wait_recv()

    @pl.when(before >= half)
    def _():
        plane(0, 0, before).wait_send()

    @pl.when(me == half)
    def _():
        plane(1, 1, 0).wait_send()
        plane(1, 2, size_px - 1).wait_send()

    for home in homes:
        home.wait()


def paired_order(length):
    counter = np.arange(length // 2)
    mirror = np.where(counter == 0, length // 2, length - counter)
    return np.stack([counter, mirror], axis=1).reshape(-1)


def kernel_path(adjoint, saved, spectra, chosen):
    size_px, size_py = lax.axis_size("px"), lax.axis_size("py")
    planes, lines, three = adjoint.shape
    one, two = planes * size_px, lines * size_py
    width, local, slots = three // size_py, spectra.shape[2], chosen.shape[0]
    whole = lambda table: pl.BlockSpec(table.shape, lambda *at: (0,) * table.ndim)
    anywhere = pl.BlockSpec(memory_space=pl.ANY)
    f32 = jnp.float32
    block = 8
    steps = planes // block
    dma = pltpu.SemaphoreType.DMA
    right_three = as_three(hartley(three), 0)
    order, half = paired_order(two), size_px // 2
    left_two = as_three(hartley(two)[order], 1)
    left_two_back = as_three(hartley(two)[:, order], 1)
    left_one = as_three(hartley(one), 1)

    field = pl.pallas_call(
        functools.partial(third_kernel, steps),
        grid=(steps,),
        in_specs=[pl.BlockSpec((block, lines, three), lambda i: (i, 0, 0)), whole(right_three)],
        out_specs=anywhere,
        out_shape=jax.ShapeDtypeStruct((size_py, planes, lines, width), f32),
        scratch_shapes=[pltpu.VMEM((size_py, planes, lines, width), f32)] + [dma((steps,))] * 3,
        compiler_params=params(collective_id=1, has_side_effects=True),
        name="third",
    )(adjoint, right_three)
    field = pl.pallas_call(
        second_kernel,
        grid=(planes // block,),
        in_specs=[
            pl.BlockSpec((size_py, block, lines, width), lambda i: (0, i, 0, 0)),
            whole(left_two),
        ],
        out_specs=pl.BlockSpec((half, 2 * local, block, width), lambda i: (0, 0, i, 0)),
        out_shape=jax.ShapeDtypeStruct((half, 2 * local, planes, width), f32),
        scratch_shapes=[pltpu.VMEM((block, two, width), f32)],
        compiler_params=params(),
        name="second",
    )(field, left_two)
    chunks = 8
    field = pl.pallas_call(
        functools.partial(middle_kernel, chunks),
        in_specs=[anywhere, anywhere, pl.BlockSpec(memory_space=pltpu.VMEM)],
        out_specs=anywhere,
        out_shape=jax.ShapeDtypeStruct((slots, half, 2 * local, planes, width), f32),
        scratch_shapes=[
            pltpu.VMEM((size_px, 2 * local, planes, width), f32),
            pltpu.VMEM((slots, one, local, width), spectra.dtype),
            pltpu.VMEM((slots, local + 2, one, width), f32),
            pltpu.VMEM((slots, half, 2 * local, planes, width), f32),
            dma((chunks, size_px)),
            dma((chunks, size_px)),
            dma((slots, chunks, half)),
            dma((slots, chunks, half)),
            dma((3,)),
            dma((2,)),
            dma,
            dma((slots,)),
            dma,
        ],
        compiler_params=params(collective_id=0, has_side_effects=True),
        name="middle",
    )(field, spectra, left_one)
    field = pl.pallas_call(
        functools.partial(second_back_kernel, slots * steps),
        grid=(slots, steps),
        in_specs=[
            pl.BlockSpec((1, half, 2 * local, block, width), lambda j, i: (j, 0, 0, i, 0)),
            whole(left_two_back),
        ],
        out_specs=anywhere,
        out_shape=jax.ShapeDtypeStruct((size_py, slots, planes, lines, width), f32),
        scratch_shapes=[
            pltpu.VMEM((block, two, width), f32),
            pltpu.VMEM((size_py, slots, planes, lines, width), f32),
        ]
        + [dma((slots * steps,))] * 3,
        compiler_params=params(collective_id=2, has_side_effects=True),
        name="second_back",
    )(field, left_two_back)
    scale = 1.0 / (one * two * three)
    piece = 4
    return pl.pallas_call(
        functools.partial(third_back_kernel, scale),
        grid=(planes // piece,),
        in_specs=[
            pl.BlockSpec(memory_space=pltpu.SMEM),
            pl.BlockSpec((size_py, slots, piece, lines, width), lambda i: (0, 0, i, 0, 0)),
            pl.BlockSpec((piece, lines, three), lambda i: (i, 0, 0)),
            whole(right_three),
        ],
        out_specs=pl.BlockSpec((piece, lines, three), lambda i: (i, 0, 0)),
        out_shape=jax.ShapeDtypeStruct((planes, lines, three), f32),
        compiler_params=params(),
        name="third_back",
    )(chosen, field, saved, right_three)


def on_device(adjoint, saved, spectra, freq_index, picked):
    chosen = chosen_index(freq_index, picked)
    width = adjoint.shape[2] // lax.axis_size("py")
    even = lax.axis_size("px") % 2 == 0 and lax.axis_size("py") == 2
    if even and adjoint.shape[0] % 8 == 0 and spectra.shape[2] % 8 == 0 and width % 128 == 0:
        return kernel_path(adjoint, saved, spectra, chosen)
    return plain_path(adjoint, saved, spectra, chosen)


def solution(mesh):
    placed = (
        P(("chain", "px"), "py", None),
        P(("chain", "px"), "py", None),
        P(None, None, "px", None),
        P(),
        P(),
    )
    return jax.shard_map(
        on_device,
        mesh=mesh,
        in_specs=placed,
        out_specs=P(("chain", "px"), "py", None),
        check_vma=False,
    )
```

profile of v0, /device:TPU:31, one launch (start us, length us, event | category | flops | bytes accessed | tf_op | source)
XLA Modules:
  0.0 283.6 jit_solution(10554497811286564924)
XLA Ops:
  0.0 7.1 %third.1.field_ref = f32[2,32,128,128]{3,2,1,0:T(8,128)} custom-call(f32[32,128,256]{2,1,0:T(8,128)} %field_ref.1, bf16[768,256]{1,0:T(8,128)(2,1)} %constant.10.clone.table_ref), custom_call_target="tpu_custom_call" | custom-call | tf_op jit(solution)/shard_map/third/pallas_call | solution.py:426
  7.1 6.0 %second.1.field_ref = f32[4,64,32,128]{3,2,1,0:T(8,128)} custom-call(f32[2,32,128,128]{3,2,1,0:T(8,128)} %third.1.field_ref, bf16[256,768]{1,0:T(8,128)(2,1)} %constant.11.clone.table_ref), custom_call_target="tpu_custom_call" | custom-call | tf_op jit(solution)/shard_map/second/pallas_call | solution.py:436
  13.1 243.8 %middle.1.field_ref = f32[2,4,64,32,128]{4,3,2,1,0:T(8,128)} custom-call(f32[4,64,32,128]{3,2,1,0:T(8,128)} %second.1.field_ref, bf16[2,256,32,256]{3,2,1,0:T(8,128)(2,1)} %spectra_ref.1, bf16[256,768]{1,0:T(8,128)(2,1)} %constant.13.clone.table_ref), custom_call_target="tpu_custom_call" | custom-call | tf_op jit(solution)/shard_map/middle/pallas_call | solution.py:450
  256.9 0.0 copy-start
  256.9 0.0 copy-start.1
  256.9 12.2 %second_back.1.field_ref = f32[2,2,32,128,128]{4,3,2,1,0:T(8,128)} custom-call(f32[2,4,64,32,128]{4,3,2,1,0:T(8,128)} %middle.1.field_ref, bf16[256,768]{1,0:T(8,128)(2,1)} %constant.12.clone.table_ref), custom_call_target="tpu_custom_call" | custom-call | tf_op jit(solution)/shard_map/second_back/pallas_call | solution.py:473
  269.1 0.0 copy-done
  269.1 0.0 copy-done.1
  269.2 0.7 fusion.chosen_ref
  269.8 13.7 %third_back.1 = f32[32,128,256]{2,1,0:T(8,128)} custom-call(s32[2]{0:T(128)} %fusion.chosen_ref, f32[2,2,32,128,128]{4,3,2,1,0:T(8,128)} %second_back.1.field_ref, f32[32,128,256]{2,1,0:T(8,128)} %saved_ref.1, bf16[768,256]{1,0:T(8,128)(2,1)} %constant.10.clone.table_ref), custom_call_target="tpu_custom_call" | custom-call | tf_op jit(solution)/shard_map/third_back/pallas_call | solution.py:492
Async XLA Ops:
  256.9 12.3 %copy-start = (s32[8]{0:T(128)S(1)}, s32[8]{0:T(128)}, u32[]{:S(2)}) copy-start(s32[8]{0:T(128)} %param.12) | copy-start | bytes 100
  256.9 12.3 %copy-start.1 = (s32[2]{0:T(128)S(1)}, s32[2]{0:T(128)}, u32[]{:S(2)}) copy-start(s32[2]{0:T(128)} %param.13) | copy-start | bytes 28
where the time goes:
time: 285 us; the launch traced here: 284 us
  Pallas kernels  283 us (99%)
    pallas_call x1, Pallas kernels, kernel_path(): pl.pallas_call(functools.partial(middle_kernel, chunks), in_specs=[anywhe...  244 us
    pallas_call x1, Pallas kernels, kernel_path(): pl.pallas_call(functools.partial(third_back_kernel, scale), grid=(planes...  13.7 us
    pallas_call x1, Pallas kernels, kernel_path(): pl.pallas_call(functools.partial(second_back_kernel, slots * steps), grid...  12.2 us
    pallas_call x1, Pallas kernels, kernel_path(): pl.pallas_call(functools.partial(third_kernel, steps), grid=(steps,), in_...  7.11 us
    pallas_call x1, Pallas kernels, kernel_path(): pl.pallas_call(second_kernel, grid=(planes // block,), in_specs=[pl.Block...  5.97 us

commit v1 on v0

--- a/solution.py
+++ b/solution.py
@@ -201,209 +201,426 @@
     chunks,
     field_ref,
     spectra_ref,
-    table_ref,
+    ahead_ref,
+    behind_ref,
     out_ref,
     gathered,
     raw,
     kernels,
     product,
-    go_send,
+    mate_send,
+    next_send,
     go_recv,
+    kernel_send,
+    kernel_recv,
+    kernel_pass,
+    extra_send,
     back_send,
     back_recv,
-    plane_send,
-    plane_recv,
+    home_sem,
     own_sem,
-    back_own,
     raw_sem,
 ):
-    half, rows_all, planes, width = field_ref.shape
-    size_px, local = 2 * half, rows_all // 2
-    slots, one = raw.shape[0], raw.shape[1]
-    step = local // chunks
+    _, rows_all, planes, width = field_ref.shape
+    size_px, slots = gathered.shape[0], raw.shape[0]
+    half, count = size_px // 2, rows_all // 2
+    held_rows, local = raw.shape[1], raw.shape[2]
+    one, middle, quarter = size_px * planes, size_px * planes // 2, local // 2
+    two = size_px * local
+    step = count // chunks
+    lead, depth, early = min(8, chunks), min(3, chunks), min(8, chunks)
     me = lax.axis_index("px")
     part = lax.axis_index("py")
+    turn_of = lax.axis_index("chain")
     lower = me < half
     base = jnp.where(lower, 0, half)
-    place = me - base
-
-    def block_of(owner):
-        return jnp.where(owner < half, owner, size_px - 1 - owner)
-
-    def other(turn):
-        return half - base + lax.rem(place + turn, half)
-
-    def mate(turn):
-        return base + lax.rem(place + turn, half)
+    column = lax.rem(me, 2)
+    mate = me + 1 - 2 * column
+    onward = jnp.where(lower, me + 2, me - 2)
+    behind = jnp.where(lower, me - 2, me + 2)
+    behind_mate = behind + 1 - 2 * column
+    inner = (me >= half - 2) & (me < half + 2)
+    outer = jnp.logical_not(inner)
+    centre = jnp.where(lower, half - 2, half)
 
     def to(index):
         return dict(device_id={"px": index}, device_id_type=pl.DeviceIdType.MESH)
 
-    def go(chunk, sender, receiver):
-        rows = pl.ds(chunk * 2 * step, 2 * step)
+    def across():
+        return dict(device_id={"chain": 1 - turn_of}, device_id_type=pl.DeviceIdType.MESH)
+
+    def rows(chunk):
+        return pl.ds(pl.multiple_of(chunk * 2 * step, 2 * step), 2 * step)
+
+    def to_mate(chunk):
         return pltpu.make_async_remote_copy(
-            src_ref=field_ref.at[block_of(receiver), rows],
-            dst_ref=gathered.at[sender, rows],
-            send_sem=go_send.at[chunk, receiver],
-            recv_sem=go_recv.at[chunk, sender],
+            src_ref=field_ref.at[1 - column, rows(chunk)],
+            dst_ref=gathered.at[me, rows(chunk)],
+            send_sem=mate_send.at[chunk],
+            recv_sem=go_recv.at[me, chunk],
+            **to(mate),
+        )
+
+    def own_on(chunk):
+        return pltpu.make_async_remote_copy(
+            src_ref=field_ref.at[column, rows(chunk)],
+            dst_ref=gathered.at[me, rows(chunk)],
+            send_sem=next_send.at[0, chunk],
+            recv_sem=go_recv.at[me, chunk],
+            **to(onward),
+        )
+
+    def pass_on(kind, owner, chunk):
+        return pltpu.make_async_remote_copy(
+            src_ref=gathered.at[owner, rows(chunk)],
+            dst_ref=gathered.at[owner, rows(chunk)],
+            send_sem=next_send.at[kind, chunk],
+            recv_sem=go_recv.at[owner, chunk],
+            **to(onward),
+        )
+
+    def back(slot, chunk, receiver):
+        return pltpu.make_async_remote_copy(
+            src_ref=product.at[slot, receiver - base, rows(chunk)],
+            dst_ref=out_ref.at[slot, column, rows(chunk)],
+            send_sem=back_send.at[slot, chunk, receiver - base],
+            recv_sem=back_recv.at[slot, chunk, column],
             **to(receiver),
         )
 
-    def back(slot, chunk, sender, receiver):
-        rows = pl.ds(chunk * 2 * step, 2 * step)
+    def back_arrival(slot, chunk, side):
         return pltpu.make_async_remote_copy(
-            src_ref=product.at[slot, receiver - base, rows],
-            dst_ref=out_ref.at[slot, block_of(sender), rows],
-            send_sem=back_send.at[slot, chunk, receiver - base],
-            recv_sem=back_recv.at[slot, chunk, sender - base],
+            src_ref=product.at[slot, 0, rows(chunk)],
+            dst_ref=out_ref.at[slot, side, rows(chunk)],
+            send_sem=back_send.at[slot, chunk, 0],
+            recv_sem=back_recv.at[slot, chunk, side],
+            **to(mate),
+        )
+
+    def home(slot, chunk):
+        return pltpu.make_async_copy(
+            product.at[slot, me - base, rows(chunk)],
+            out_ref.at[slot, column, rows(chunk)],
+            home_sem.at[slot, chunk],
+        )
+
+    def frequency(place):
+        group, at = lax.div(place, count // 2), lax.rem(place, count // 2)
+        block = 2 - 2 * group + lax.rem(at, 2)
+        return local * block + quarter - 1 - lax.div(at, 2) + quarter * column
+
+    def source(place):
+        value = jnp.where(place == count, two // 2, frequency(place))
+        above = jnp.where(value == 0, 0, lax.div(two - value, local))
+        holder = jnp.where(lower, lax.div(value, local), above)
+        row = jnp.where(lower | (value == 0), lax.rem(value, local), lax.rem(two - value, local))
+        return jnp.where(place == count, half, holder), row
+
+    def held_at(place):
+        holder, row = source(place)
+        return jnp.where(holder == me, count + 1 + row, place)
+
+    def firsthand(place):
+        return lax.rem(lax.div(place, 2), 2) == turn_of
+
+    def kernel_row(turn):
+        offset = quarter - 1 - lax.div(turn, 2) + quarter * lax.rem(turn, 2)
+        row = jnp.where(lower, offset, lax.rem(local - offset, local))
+        value = jnp.where(lower, local * me + row, two - local * me - row)
+        block, inside = lax.div(value, local), lax.rem(value, local)
+        side, level = lax.div(inside, quarter), lax.rem(inside, quarter)
+        place = jnp.where(block >= 2, 0, count // 2) + 2 * (quarter - 1 - level) + lax.rem(block, 2)
+        return row, side, jnp.where(value == two // 2, count, place)
+
+    def kernel_copy(row, place, receiver, sem):
+        return pltpu.make_async_remote_copy(
+            src_ref=kernels.at[count + 1 + row],
+            dst_ref=kernels.at[place],
+            send_sem=sem,
+            recv_sem=kernel_recv.at[place],
             **to(receiver),
         )
 
-    def plane(kind, send, receiver):
+    def each_kernel_row(turn, act):
+        row, side, place = kernel_row(turn)
+
+        @pl.when((centre + side != me) & firsthand(place))
+        def _():
+            act(kernel_copy(row, place, centre + side, kernel_send.at[row]))
+
+    def extra_copy(act):
+        for sender, place, receiver in ((0, count - 2, half), (half, count, half - 2)):
+
+            @pl.when((me == sender) & firsthand(jnp.int32(place)))
+            def _():
+                act(kernel_copy(0, place, jnp.int32(receiver), extra_send))
+
+    def kernel_arrival(place):
+        return kernel_copy(0, place, mate, extra_send)
+
+    def kernel_on(place):
         return pltpu.make_async_remote_copy(
-            src_ref=kernels.at[:, 0],
-            dst_ref=kernels.at[:, local + kind],
-            send_sem=plane_send.at[send],
-            recv_sem=plane_recv.at[kind],
-            **to(receiver),
-        )
-
-    own = pltpu.make_async_copy(field_ref.at[block_of(me)], gathered.at[me], own_sem)
-    fetch = pltpu.make_async_copy(spectra_ref.at[:, :, :, pl.ds(part * width, width)], raw, raw_sem)
-    own.start()
+            src_ref=kernels.at[place],
+            dst_ref=kernels.at[place],
+            send_sem=kernel_pass.at[place],
+            recv_sem=kernel_recv.at[place],
+            **across(),
+        )
+
+    def arrives(place):
+        return source(place)[0] != me
+
+    leading_place = count - 2
+
+    def pass_kernel(place):
+        @pl.when(arrives(place) & firsthand(place))
+        def _():
+            kernel_arrival(place).wait_recv()
+            kernel_on(place).start()
+
+    def await_kernel(place):
+        @pl.when(arrives(place) & jnp.logical_not(firsthand(place)))
+        def _():
+            kernel_arrival(place).wait_recv()
+
+    def with_last(chunk, act):
+        @pl.when((chunk == leading_place // step) & (column == 0))
+        def _():
+            act(jnp.int32(count))
+
+    own = pltpu.make_async_copy(field_ref.at[column], gathered.at[me], own_sem)
+    fetch = pltpu.make_async_copy(
+        spectra_ref.at[:, pl.ds(0, held_rows), :, pl.ds(part * width, width)], raw, raw_sem
+    )
     fetch.start()
 
+    @pl.when(inner)
+    def _():
+        own.start()
+
     barrier = pltpu.get_barrier_semaphore()
-
-    @pl.loop(1, size_px)
+    everyone = 2 * size_px
+
+    @pl.loop(1, everyone)
     def _(turn):
-        pl.semaphore_signal(barrier, inc=1, **to(lax.rem(me + turn, size_px)))
-
-    pl.semaphore_wait(barrier, size_px - 1)
-
-    def send_chunk(at):
-        chunk = chunks - 1 - at
-
-        @pl.loop(0, half)
-        def _(turn):
-            go(chunk, me, other(turn)).start()
-
-        @pl.loop(1, half)
-        def _(turn):
-            go(chunk, me, mate(turn)).start()
-
-    early = chunks // 2
-    pl.loop(0, early)(send_chunk)
-    own.wait()
-    fetch.wait()
-    block = 16
-
-    @pl.loop(0, one // block)
-    def _(at):
-        rows = pl.ds(pl.multiple_of(at * block, block), block)
+        peer = lax.rem(turn_of * size_px + me + turn, everyone)
+        pl.semaphore_signal(
+            barrier,
+            inc=1,
+            device_id={"chain": lax.div(peer, size_px), "px": lax.rem(peer, size_px)},
+            device_id_type=pl.DeviceIdType.MESH,
+        )
+
+    pl.semaphore_wait(barrier, everyone - 1)
+
+    def send_own(chunk):
+        own_on(chunk).start()
+        to_mate(chunk).start()
+
+    def convert():
+        fetch.wait()
+        block = 16
         for slot in range(slots):
-            piece = raw[slot, rows].astype(jnp.float32)
-            kernels[slot, 0:local, rows, :] = jnp.swapaxes(piece, 0, 1)
-
-    before = lax.rem(me + size_px - 1, size_px)
-    ends = (me == 0) | (me == size_px - 1)
-
-    @pl.when(before >= half)
-    def _():
-        plane(0, 0, before).start()
-
-    @pl.when(me == half)
-    def _():
-        plane(1, 1, 0).start()
-        plane(1, 2, size_px - 1).start()
-
-    pl.loop(early, chunks)(send_chunk)
-
-    @pl.loop(0, chunks)
-    def _(at):
-        chunk = chunks - 1 - at
-
-        @pl.loop(0, half)
-        def _(turn):
-            go(chunk, other(turn), me).wait_recv()
-
-        @pl.loop(1, half)
-        def _(turn):
-            go(chunk, mate(turn), me).wait_recv()
-
-        @pl.when(chunk == 0)
-        def _():
-            @pl.when(jnp.logical_not(lower))
-            def _():
-                plane(0, 0, before).wait_recv()
-
-            @pl.when(ends)
-            def _():
-                plane(1, 1, before).wait_recv()
-
+
+            @pl.loop(0, middle // block)
+            def _(at):
+                span = pl.ds(pl.multiple_of(at * block, block), block)
+                piece = raw[slot, span].astype(jnp.float32)
+                kernels[count + 1 :, slot, span, :] = jnp.swapaxes(piece, 0, 1)
+
+            piece = raw[slot, middle : middle + block].astype(jnp.float32)
+            kernels[count + 1 :, slot, middle : middle + 8, :] = jnp.swapaxes(piece[:8], 0, 1)
+
+    def relay(chunk):
+        pass_on(1, mate, chunk).wait_recv()
+        pass_on(1, mate, chunk).start()
+
+        @pl.when(inner)
+        def _():
+            for kind, owner in ((2, behind), (3, behind_mate)):
+                pass_on(kind, owner, chunk).wait_recv()
+                pass_on(kind, owner, chunk).start()
+
+        @pl.when(chunk + lead < chunks)
+        def _():
+            send_own(chunk + lead)
+
+    def relay_kernels(chunk):
+        @pl.loop(0, step)
+        def _(at):
+            pass_kernel(chunk * step + at)
+
+        with_last(chunk, pass_kernel)
+
+    def compute(chunk):
+        for owner in (onward, onward + 1 - 2 * column):
+            pass_on(1, owner, chunk).wait_recv()
+        further = jnp.where(lower, onward + 2, onward - 2)
+        for owner in (further, further + 1 - 2 * column):
+            pass_on(1, owner, chunk).wait_recv()
+
+        @pl.loop(0, step)
+        def _(at):
+            await_kernel(chunk * step + at)
+
+        with_last(chunk, await_kernel)
         own_sites = pl.ds(pl.multiple_of(base * planes, half * planes), half * planes)
+        top = lax.broadcasted_iota(jnp.int32, (middle, 2 * width), 0) == 0
 
         @pl.loop(0, step)
-        def _(inner):
-            line = chunk * step + inner
+        def _(at):
+            line = chunk * step + at
             first, second = 2 * line, 2 * line + 1
             columns = jnp.concatenate(
-                [gathered[:, at].reshape(one, width) for at in (first, second)], axis=1
+                [gathered[:, row].reshape(one, width) for row in (first, second)], axis=1
             )
-            spectrum = from_left(table_ref[...], columns)
-            leading = line == 0
-            plain = jnp.where(lower, line, local - line)
-            mirrored = jnp.where(leading & ends, local + 1, plain)
+            spectrum = from_left(ahead_ref[...], columns)
+            plain = held_at(line)
+            leading = (line == leading_place) & (column == 0)
+            mirrored = jnp.where(leading, held_at(jnp.int32(count)), plain)
             for slot in range(slots):
-                factor = jnp.concatenate([kernels[slot, plain], kernels[slot, mirrored]], axis=1)
-                result = from_left(table_ref[own_sites, :], spectrum * factor)
+                body = jnp.concatenate(
+                    [kernels[plain, slot, 0:middle], kernels[mirrored, slot, 0:middle]], axis=1
+                )
+                edge = jnp.concatenate(
+                    [
+                        kernels[plain, slot, middle : middle + 1],
+                        kernels[mirrored, slot, middle : middle + 1],
+                    ],
+                    axis=1,
+                )
+                factor = jnp.concatenate([body, jnp.where(top, edge, body)], axis=0)
+                result = from_left(behind_ref[own_sites, :], spectrum * factor)
                 product[slot, :, first] = result[:, :width].reshape(half, planes, width)
                 product[slot, :, second] = result[:, width:].reshape(half, planes, width)
 
         for slot in range(slots):
 
-            @pl.loop(1, half)
+            @pl.loop(0, half)
             def _(turn):
-                back(slot, chunk, me, mate(turn)).start()
-
-    homes = [
-        pltpu.make_async_copy(
-            product.at[slot, place], out_ref.at[slot, block_of(me)], back_own.at[slot]
-        )
-        for slot in range(slots)
-    ]
-    for home in homes:
-        home.start()
+                receiver = base + turn
+
+                @pl.when(receiver != me)
+                def _():
+                    back(slot, chunk, receiver).start()
+
+            home(slot, chunk).start()
+
+    pl.loop(0, lead)(send_own)
+
+    @pl.when(inner)
+    def _():
+        convert()
+        extra_copy(lambda copy: copy.start())
+
+        @pl.loop(0, local)
+        def _(turn):
+            each_kernel_row(turn, lambda copy: copy.start())
+
+        own.wait()
+
+        @pl.loop(0, depth)
+        def _(chunk):
+            relay(chunk)
+            relay_kernels(chunk)
+
+        @pl.loop(0, chunks)
+        def _(chunk):
+            @pl.when(chunk + depth < chunks)
+            def _():
+                relay(chunk + depth)
+                relay_kernels(chunk + depth)
+
+            compute(chunk)
+
+    @pl.when(outer)
+    def _():
+        pl.loop(0, early)(relay)
+        convert()
+        extra_copy(lambda copy: copy.start())
+        late = chunks - early
+        pace = -(-local // max(late, 1))
+
+        @pl.loop(early, chunks)
+        def _(chunk):
+            relay(chunk)
+
+            @pl.loop(0, pace)
+            def _(at):
+                turn = (chunk - early) * pace + at
+
+                @pl.when(turn < local)
+                def _():
+                    each_kernel_row(turn, lambda copy: copy.start())
+
+        if late == 0:
+
+            @pl.loop(0, local)
+            def _(turn):
+                each_kernel_row(turn, lambda copy: copy.start())
 
     @pl.loop(0, chunks)
     def _(chunk):
-        @pl.loop(1, size_px)
-        def _(turn):
-            go(chunk, me, lax.rem(me + turn, size_px)).wait_send()
-
-        @pl.loop(1, half)
-        def _(turn):
+        to_mate(chunk).wait_send()
+        own_on(chunk).wait_send()
+        pass_on(1, mate, chunk).wait_send()
+        for slot in range(slots):
+            back_arrival(slot, chunk, 1 - column).wait_recv()
+
+        @pl.when(outer)
+        def _():
             for slot in range(slots):
-                back(slot, chunk, me, mate(turn)).wait_send()
-                back(slot, chunk, mate(turn), me).wait_recv()
-
-    @pl.when(before >= half)
+                back_arrival(slot, chunk, column).wait_recv()
+
+        @pl.when(inner)
+        def _():
+            for kind, owner in ((2, behind), (3, behind_mate)):
+                pass_on(kind, owner, chunk).wait_send()
+            for slot in range(slots):
+                home(slot, chunk).wait()
+
+                @pl.loop(0, half)
+                def _(turn):
+                    receiver = base + turn
+
+                    @pl.when(receiver != me)
+                    def _():
+                        back(slot, chunk, receiver).wait_send()
+
+    @pl.loop(0, local)
+    def _(turn):
+        each_kernel_row(turn, lambda copy: copy.wait_send())
+
+    extra_copy(lambda copy: copy.wait_send())
+
+    @pl.when(inner)
     def _():
-        plane(0, 0, before).wait_send()
-
-    @pl.when(me == half)
-    def _():
-        plane(1, 1, 0).wait_send()
-        plane(1, 2, size_px - 1).wait_send()
-
-    for home in homes:
-        home.wait()
-
-
-def paired_order(length):
+        def passed(place):
+            @pl.when(arrives(place) & firsthand(place))
+            def _():
+                kernel_on(place).wait_send()
+
+        pl.loop(0, count)(passed)
+
+        @pl.when(column == 0)
+        def _():
+            passed(jnp.int32(count))
+
+
+def second_order(length, blocks):
+    count, local = length // 4, length // (2 * blocks)
+    quarter = local // 2
+    side, place = np.divmod(np.arange(2 * count), count)
+    group, at = np.divmod(place, count // 2)
+    block = 2 - 2 * group + at % 2
+    value = local * block + quarter - 1 - at // 2 + quarter * side
+    mirror = np.where(value == 0, length // 2, length - value)
+    return np.stack([value, mirror], axis=1).reshape(-1)
+
+
+def first_order(length):
     counter = np.arange(length // 2)
-    mirror = np.where(counter == 0, length // 2, length - counter)
-    return np.stack([counter, mirror], axis=1).reshape(-1)
+    return np.concatenate([counter, np.where(counter == 0, length // 2, length - counter)])
 
 
 def kernel_path(adjoint, saved, spectra, chosen):
@@ -418,10 +635,13 @@
     steps = planes // block
     dma = pltpu.SemaphoreType.DMA
     right_three = as_three(hartley(three), 0)
-    order, half = paired_order(two), size_px // 2
+    half = size_px // 2
+    order = second_order(two, half)
+    order_one = first_order(one)
     left_two = as_three(hartley(two)[order], 1)
     left_two_back = as_three(hartley(two)[:, order], 1)
-    left_one = as_three(hartley(one), 1)
+    left_one = as_three(hartley(one)[order_one], 1)
+    left_one_back = as_three(hartley(one)[:, order_one], 1)
 
     field = pl.pallas_call(
         functools.partial(third_kernel, steps),
@@ -440,41 +660,46 @@
             pl.BlockSpec((size_py, block, lines, width), lambda i: (0, i, 0, 0)),
             whole(left_two),
         ],
-        out_specs=pl.BlockSpec((half, 2 * local, block, width), lambda i: (0, 0, i, 0)),
-        out_shape=jax.ShapeDtypeStruct((half, 2 * local, planes, width), f32),
+        out_specs=pl.BlockSpec((2, two // 2, block, width), lambda i: (0, 0, i, 0)),
+        out_shape=jax.ShapeDtypeStruct((2, two // 2, planes, width), f32),
         scratch_shapes=[pltpu.VMEM((block, two, width), f32)],
         compiler_params=params(),
         name="second",
     )(field, left_two)
-    chunks = 8
+    chunks = 32
+    count = two // 4
+    in_vmem = pl.BlockSpec(memory_space=pltpu.VMEM)
     field = pl.pallas_call(
         functools.partial(middle_kernel, chunks),
-        in_specs=[anywhere, anywhere, pl.BlockSpec(memory_space=pltpu.VMEM)],
+        in_specs=[anywhere, anywhere, in_vmem, in_vmem],
         out_specs=anywhere,
-        out_shape=jax.ShapeDtypeStruct((slots, half, 2 * local, planes, width), f32),
+        out_shape=jax.ShapeDtypeStruct((slots, 2, two // 2, planes, width), f32),
         scratch_shapes=[
-            pltpu.VMEM((size_px, 2 * local, planes, width), f32),
-            pltpu.VMEM((slots, one, local, width), spectra.dtype),
-            pltpu.VMEM((slots, local + 2, one, width), f32),
-            pltpu.VMEM((slots, half, 2 * local, planes, width), f32),
-            dma((chunks, size_px)),
-            dma((chunks, size_px)),
+            pltpu.VMEM((size_px, two // 2, planes, width), f32),
+            pltpu.VMEM((slots, one // 2 + 16, local, width), spectra.dtype),
+            pltpu.VMEM((count + 1 + local, slots, one // 2 + 8, width), f32),
+            pltpu.VMEM((slots, half, two // 2, planes, width), f32),
+            dma((chunks,)),
+            dma((4, chunks)),
+            dma((size_px, chunks)),
+            dma((local,)),
+            dma((count + 1,)),
+            dma((count + 1,)),
+            dma,
             dma((slots, chunks, half)),
-            dma((slots, chunks, half)),
-            dma((3,)),
-            dma((2,)),
+            dma((slots, chunks, 2)),
+            dma((slots, chunks)),
             dma,
-            dma((slots,)),
             dma,
         ],
         compiler_params=params(collective_id=0, has_side_effects=True),
         name="middle",
-    )(field, spectra, left_one)
+    )(field, spectra, left_one, left_one_back)
     field = pl.pallas_call(
         functools.partial(second_back_kernel, slots * steps),
         grid=(slots, steps),
         in_specs=[
-            pl.BlockSpec((1, half, 2 * local, block, width), lambda j, i: (j, 0, 0, i, 0)),
+            pl.BlockSpec((1, 2, two // 2, block, width), lambda j, i: (j, 0, 0, i, 0)),
             whole(left_two_back),
         ],
         out_specs=anywhere,
@@ -508,8 +733,8 @@
 def on_device(adjoint, saved, spectra, freq_index, picked):
     chosen = chosen_index(freq_index, picked)
     width = adjoint.shape[2] // lax.axis_size("py")
-    even = lax.axis_size("px") % 2 == 0 and lax.axis_size("py") == 2
-    if even and adjoint.shape[0] % 8 == 0 and spectra.shape[2] % 8 == 0 and width % 128 == 0:
+    even = lax.axis_size("px") == 8 and lax.axis_size("py") == 2 and lax.axis_size("chain") == 2
+    if even and adjoint.shape[0] % 8 == 0 and spectra.shape[2] % 32 == 0 and width % 128 == 0:
         return kernel_path(adjoint, saved, spectra, chosen)
     return plain_path(adjoint, saved, spectra, chosen)
 

time: 285 us -> 293 us (1.028)
  Pallas kernels: 283 us -> 291 us
    pallas_call x1, Pallas kernels: 244 us -> 250 us  [kernel_path(): pl.pallas_call(functools.partial(middle_kernel, chunks), in_specs=[anywhe...]
where the time goes in v1:
time: 293 us; the launch traced here: 292 us
  Pallas kernels  291 us (99%)
    pallas_call x1, Pallas kernels, kernel_path(): pl.pallas_call(functools.partial(middle_kernel, chunks), in_specs=[anywhe...  250 us
    pallas_call x1, Pallas kernels, kernel_path(): pl.pallas_call(functools.partial(second_back_kernel, slots * steps), grid...  13.9 us
    pallas_call x1, Pallas kernels, kernel_path(): pl.pallas_call(functools.partial(third_back_kernel, scale), grid=(planes...  13.7 us
    pallas_call x1, Pallas kernels, kernel_path(): pl.pallas_call(functools.partial(third_kernel, steps), grid=(steps,), in_...  7.11 us
    pallas_call x1, Pallas kernels, kernel_path(): pl.pallas_call(second_kernel, grid=(planes // block,), in_specs=[pl.Block...  5.97 us

profile of v1, /device:TPU:31, one launch (start us, length us, event | category | flops | bytes accessed | tf_op | source)
XLA Modules:
  0.0 291.9 jit_solution(12719601634944266818)
XLA Ops:
  0.0 7.1 %third.1.field_ref = f32[2,32,128,128]{3,2,1,0:T(8,128)} custom-call(f32[32,128,256]{2,1,0:T(8,128)} %field_ref.1, bf16[768,256]{1,0:T(8,128)(2,1)} %constant.12.clone.table_ref), custom_call_target="tpu_custom_call" | custom-call | tf_op jit(solution)/shard_map/third/pallas_call | solution.py:646
  7.1 6.0 %second.1.field_ref = f32[2,128,32,128]{3,2,1,0:T(8,128)} custom-call(f32[2,32,128,128]{3,2,1,0:T(8,128)} %third.1.field_ref, bf16[256,768]{1,0:T(8,128)(2,1)} %constant.13.clone.table_ref), custom_call_target="tpu_custom_call" | custom-call | tf_op jit(solution)/shard_map/second/pallas_call | solution.py:656
  13.1 250.4 %middle.1.field_ref = f32[2,2,128,32,128]{4,3,2,1,0:T(8,128)} custom-call(f32[2,128,32,128]{3,2,1,0:T(8,128)} %second.1.field_ref, bf16[2,256,32,256]{3,2,1,0:T(8,128)(2,1)} %spectra_ref.1, bf16[256,768]{1,0:T(8,128)(2,1)} %constant.15.clone.ahead_ref, bf16[256,768]{1,0:T(8,128)(2,1)} %constant.16.clone.behind_ref), custom_call_target="tpu_custom_call" | custom-call | tf_op jit(solution)/shard_map/middle/pallas_call | solution.py:672
  263.5 0.0 copy-start
  263.5 0.0 copy-start.1
  263.5 13.9 %second_back.1.field_ref = f32[2,2,32,128,128]{4,3,2,1,0:T(8,128)} custom-call(f32[2,2,128,32,128]{4,3,2,1,0:T(8,128)} %middle.1.field_ref, bf16[256,768]{1,0:T(8,128)(2,1)} %constant.14.clone.table_ref), custom_call_target="tpu_custom_call" | custom-call | tf_op jit(solution)/shard_map/second_back/pallas_call | solution.py:698
  277.4 0.0 copy-done
  277.5 0.0 copy-done.1
  277.5 0.7 fusion.chosen_ref
  278.1 13.7 %third_back.1 = f32[32,128,256]{2,1,0:T(8,128)} custom-call(s32[2]{0:T(128)} %fusion.chosen_ref, f32[2,2,32,128,128]{4,3,2,1,0:T(8,128)} %second_back.1.field_ref, f32[32,128,256]{2,1,0:T(8,128)} %saved_ref.1, bf16[768,256]{1,0:T(8,128)(2,1)} %constant.12.clone.table_ref), custom_call_target="tpu_custom_call" | custom-call | tf_op jit(solution)/shard_map/third_back/pallas_call | solution.py:717
Async XLA Ops:
  263.5 14.0 %copy-start = (s32[8]{0:T(128)S(1)}, s32[8]{0:T(128)}, u32[]{:S(2)}) copy-start(s32[8]{0:T(128)} %param.13) | copy-start | bytes 100
  263.5 14.0 %copy-start.1 = (s32[2]{0:T(128)S(1)}, s32[2]{0:T(128)}, u32[]{:S(2)}) copy-start(s32[2]{0:T(128)} %param.14) | copy-start | bytes 28

commit v2 on v1

--- a/solution.py
+++ b/solution.py
@@ -228,7 +228,10 @@
     one, middle, quarter = size_px * planes, size_px * planes // 2, local // 2
     two = size_px * local
     step = count // chunks
-    lead, depth, early = min(8, chunks), min(3, chunks), min(8, chunks)
+    lead, depth, early = 2, 1, min(10, chunks // 2)
+    per_chunk = -(-2 * local // chunks)
+    first_rows = min(local, 4 * per_chunk)
+    pace = -(-local // (chunks - early)) + 0
     me = lax.axis_index("px")
     part = lax.axis_index("py")
     turn_of = lax.axis_index("chain")
@@ -324,6 +327,7 @@
         return lax.rem(lax.div(place, 2), 2) == turn_of
 
     def kernel_row(turn):
+        turn = jnp.where(lower, turn, lax.rem(turn + local - 2, local))
         offset = quarter - 1 - lax.div(turn, 2) + quarter * lax.rem(turn, 2)
         row = jnp.where(lower, offset, lax.rem(local - offset, local))
         value = jnp.where(lower, local * me + row, two - local * me - row)
@@ -506,6 +510,13 @@
 
             home(slot, chunk).start()
 
+    def send_kernels(begin, length):
+        @pl.loop(0, length)
+        def _(at):
+            @pl.when(begin + at < local)
+            def _():
+                each_kernel_row(begin + at, lambda copy: copy.start())
+
     pl.loop(0, lead)(send_own)
 
     @pl.when(inner)
@@ -513,10 +524,7 @@
         convert()
         extra_copy(lambda copy: copy.start())
 
-        @pl.loop(0, local)
-        def _(turn):
-            each_kernel_row(turn, lambda copy: copy.start())
-
+        send_kernels(jnp.int32(0), first_rows)
         own.wait()
 
         @pl.loop(0, depth)
@@ -526,6 +534,8 @@
 
         @pl.loop(0, chunks)
         def _(chunk):
+            send_kernels(first_rows + chunk * per_chunk, per_chunk)
+
             @pl.when(chunk + depth < chunks)
             def _():
                 relay(chunk + depth)
@@ -538,26 +548,11 @@
         pl.loop(0, early)(relay)
         convert()
         extra_copy(lambda copy: copy.start())
-        late = chunks - early
-        pace = -(-local // max(late, 1))
 
         @pl.loop(early, chunks)
         def _(chunk):
             relay(chunk)
-
-            @pl.loop(0, pace)
-            def _(at):
-                turn = (chunk - early) * pace + at
-
-                @pl.when(turn < local)
-                def _():
-                    each_kernel_row(turn, lambda copy: copy.start())
-
-        if late == 0:
-
-            @pl.loop(0, local)
-            def _(turn):
-                each_kernel_row(turn, lambda copy: copy.start())
+            send_kernels((chunk - early) * pace, pace)
 
     @pl.loop(0, chunks)
     def _(chunk):

time: 293 us -> 261 us (0.89)
  Pallas kernels: 291 us -> 256 us
    pallas_call x1, Pallas kernels: 250 us -> 214 us  [kernel_path(): pl.pallas_call(functools.partial(middle_kernel, chunks), in_specs=[anywhe...]
where the time goes in v2:
time: 261 us; the launch traced here: 257 us
  Pallas kernels  256 us (98%)
    pallas_call x1, Pallas kernels, kernel_path(): pl.pallas_call(functools.partial(middle_kernel, chunks), in_specs=[anywhe...  214 us
    pallas_call x1, Pallas kernels, kernel_path(): pl.pallas_call(functools.partial(second_back_kernel, slots * steps), grid...  15.7 us
    pallas_call x1, Pallas kernels, kernel_path(): pl.pallas_call(functools.partial(third_back_kernel, scale), grid=(planes...  13.7 us
    pallas_call x1, Pallas kernels, kernel_path(): pl.pallas_call(functools.partial(third_kernel, steps), grid=(steps,), in_...  7.11 us
    pallas_call x1, Pallas kernels, kernel_path(): pl.pallas_call(second_kernel, grid=(planes // block,), in_specs=[pl.Block...  5.97 us

profile of v2, /device:TPU:31, one launch (start us, length us, event | category | flops | bytes accessed | tf_op | source)
XLA Modules:
  0.0 257.2 jit_solution(229067527960545616)
XLA Ops:
  0.0 7.1 %third.1.field_ref = f32[2,32,128,128]{3,2,1,0:T(8,128)} custom-call(f32[32,128,256]{2,1,0:T(8,128)} %field_ref.1, bf16[768,256]{1,0:T(8,128)(2,1)} %constant.12.clone.table_ref), custom_call_target="tpu_custom_call" | custom-call | tf_op jit(solution)/shard_map/third/pallas_call | solution.py:641
  7.1 6.0 %second.1.field_ref = f32[2,128,32,128]{3,2,1,0:T(8,128)} custom-call(f32[2,32,128,128]{3,2,1,0:T(8,128)} %third.1.field_ref, bf16[256,768]{1,0:T(8,128)(2,1)} %constant.13.clone.table_ref), custom_call_target="tpu_custom_call" | custom-call | tf_op jit(solution)/shard_map/second/pallas_call | solution.py:651
  13.1 213.9 %middle.1.field_ref = f32[2,2,128,32,128]{4,3,2,1,0:T(8,128)} custom-call(f32[2,128,32,128]{3,2,1,0:T(8,128)} %second.1.field_ref, bf16[2,256,32,256]{3,2,1,0:T(8,128)(2,1)} %spectra_ref.1, bf16[256,768]{1,0:T(8,128)(2,1)} %constant.15.clone.ahead_ref, bf16[256,768]{1,0:T(8,128)(2,1)} %constant.16.clone.behind_ref), custom_call_target="tpu_custom_call" | custom-call | tf_op jit(solution)/shard_map/middle/pallas_call | solution.py:667
  227.0 0.0 copy-start
  227.0 0.0 copy-start.1
  227.0 15.7 %second_back.1.field_ref = f32[2,2,32,128,128]{4,3,2,1,0:T(8,128)} custom-call(f32[2,2,128,32,128]{4,3,2,1,0:T(8,128)} %middle.1.field_ref, bf16[256,768]{1,0:T(8,128)(2,1)} %constant.14.clone.table_ref), custom_call_target="tpu_custom_call" | custom-call | tf_op jit(solution)/shard_map/second_back/pallas_call | solution.py:693
  242.7 0.0 copy-done
  242.8 0.0 copy-done.1
  242.8 0.7 fusion.chosen_ref
  243.4 13.7 %third_back.1 = f32[32,128,256]{2,1,0:T(8,128)} custom-call(s32[2]{0:T(128)} %fusion.chosen_ref, f32[2,2,32,128,128]{4,3,2,1,0:T(8,128)} %second_back.1.field_ref, f32[32,128,256]{2,1,0:T(8,128)} %saved_ref.1, bf16[768,256]{1,0:T(8,128)(2,1)} %constant.12.clone.table_ref), custom_call_target="tpu_custom_call" | custom-call | tf_op jit(solution)/shard_map/third_back/pallas_call | solution.py:712
Async XLA Ops:
  227.0 15.8 %copy-start = (s32[8]{0:T(128)S(1)}, s32[8]{0:T(128)}, u32[]{:S(2)}) copy-start(s32[8]{0:T(128)} %param.13) | copy-start | bytes 100
  227.0 15.8 %copy-start.1 = (s32[2]{0:T(128)S(1)}, s32[2]{0:T(128)}, u32[]{:S(2)}) copy-start(s32[2]{0:T(128)} %param.14) | copy-start | bytes 28

commit v3 on v2

--- a/solution.py
+++ b/solution.py
@@ -150,6 +150,15 @@
         out_ref[peer] = jnp.swapaxes(held[:, peer * local : (peer + 1) * local, :], 0, 1)
 
 
+def cosine_turns(turns):
+    turns = turns - jnp.floor(turns + 0.5)
+    square = turns * turns * (4.0 * math.pi * math.pi)
+    value = jnp.full_like(square, 1.0 / math.factorial(20))
+    for order in range(9, -1, -1):
+        value = value * square + (-1.0) ** order / math.factorial(2 * order)
+    return value
+
+
 def second_back_kernel(steps, field_ref, table_ref, out_ref, held, mine, *sems):
     _, groups, local, planes, width = field_ref.shape
     parts, lines = mine.shape[0], mine.shape[3]
@@ -174,36 +183,31 @@
     core_exchange(step, steps, block(mine), block(out_ref), sems)
 
 
-def cosine_turns(turns):
-    turns = turns - jnp.floor(turns + 0.5)
-    square = turns * turns * (4.0 * math.pi * math.pi)
-    value = jnp.full_like(square, 1.0 / math.factorial(20))
-    for order in range(9, -1, -1):
-        value = value * square + (-1.0) ** order / math.factorial(2 * order)
-    return value
-
-
-def third_back_kernel(scale, chosen_ref, field_ref, saved_ref, table_ref, out_ref):
+def third_back_kernel(field_ref, weight_ref, table_ref, out_ref):
     parts, slots, planes, lines, width = field_ref.shape
     three = parts * width
     total = None
-    site = saved_ref[...].reshape(planes * lines, three)
     for slot in range(slots):
         sides = [field_ref[part, slot].reshape(planes * lines, width) for part in range(parts)]
         field = from_right(jnp.concatenate(sides, axis=1), table_ref[...])
-        index = chosen_ref[slot].astype(jnp.float32)
-        weight = cosine_turns(site * (index * (1.0 / 16.0))) * (index * (math.pi / 8.0 * scale))
-        total = weight * field if total is None else total + weight * field
+        term = weight_ref[slot].reshape(planes * lines, three) * field
+        total = term if total is None else total + term
     out_ref[...] = total.reshape(planes, lines, three)
 
 
 def middle_kernel(
     chunks,
+    scale,
+    chosen_ref,
     field_ref,
     spectra_ref,
+    saved_ref,
     ahead_ref,
     behind_ref,
     out_ref,
+    weight_ref,
+    site,
+    weighed,
     gathered,
     raw,
     kernels,
@@ -220,6 +224,8 @@
     home_sem,
     own_sem,
     raw_sem,
+    site_sem,
+    weigh_sem,
 ):
     _, rows_all, planes, width = field_ref.shape
     size_px, slots = gathered.shape[0], raw.shape[0]
@@ -396,6 +402,7 @@
     fetch = pltpu.make_async_copy(
         spectra_ref.at[:, pl.ds(0, held_rows), :, pl.ds(part * width, width)], raw, raw_sem
     )
+    sites = pltpu.make_async_copy(saved_ref, site, site_sem)
     fetch.start()
 
     @pl.when(inner)
@@ -434,6 +441,27 @@
 
             piece = raw[slot, middle : middle + block].astype(jnp.float32)
             kernels[count + 1 :, slot, middle : middle + 8, :] = jnp.swapaxes(piece[:8], 0, 1)
+
+    span = planes // chunks
+
+    def weights_out(chunk):
+        return pltpu.make_async_copy(
+            weighed.at[lax.rem(chunk, 2)],
+            weight_ref.at[:, pl.ds(chunk * span, span)],
+            weigh_sem.at[chunk],
+        )
+
+    def weigh(chunk):
+        @pl.when(chunk >= 2)
+        def _():
+            weights_out(chunk - 2).wait()
+
+        for slot in range(slots):
+            index = chosen_ref[slot].astype(jnp.float32)
+            turns = site[pl.ds(chunk * span, span)] * (index * (1.0 / 16.0))
+            value = cosine_turns(turns) * (index * (math.pi / 8.0 * scale))
+            weighed[lax.rem(chunk, 2), slot] = value
+        weights_out(chunk).start()
 
     def relay(chunk):
         pass_on(1, mate, chunk).wait_recv()
@@ -526,12 +554,15 @@
 
         send_kernels(jnp.int32(0), first_rows)
         own.wait()
+        sites.start()
 
         @pl.loop(0, depth)
         def _(chunk):
             relay(chunk)
             relay_kernels(chunk)
 
+        sites.wait()
+
         @pl.loop(0, chunks)
         def _(chunk):
             send_kernels(first_rows + chunk * per_chunk, per_chunk)
@@ -541,11 +572,13 @@
                 relay(chunk + depth)
                 relay_kernels(chunk + depth)
 
+            weigh(chunk)
             compute(chunk)
 
     @pl.when(outer)
     def _():
         pl.loop(0, early)(relay)
+        sites.start()
         convert()
         extra_copy(lambda copy: copy.start())
 
@@ -553,6 +586,9 @@
         def _(chunk):
             relay(chunk)
             send_kernels((chunk - early) * pace, pace)
+
+        sites.wait()
+        pl.loop(0, chunks)(weigh)
 
     @pl.loop(0, chunks)
     def _(chunk):
@@ -581,6 +617,10 @@
                     @pl.when(receiver != me)
                     def _():
                         back(slot, chunk, receiver).wait_send()
+
+    @pl.loop(chunks - 2, chunks)
+    def _(chunk):
+        weights_out(chunk).wait()
 
     @pl.loop(0, local)
     def _(turn):
@@ -635,6 +675,7 @@
     order_one = first_order(one)
     left_two = as_three(hartley(two)[order], 1)
     left_two_back = as_three(hartley(two)[:, order], 1)
+    scale = 1.0 / (one * two * three)
     left_one = as_three(hartley(one)[order_one], 1)
     left_one_back = as_three(hartley(one)[:, order_one], 1)
 
@@ -661,15 +702,20 @@
         compiler_params=params(),
         name="second",
     )(field, left_two)
-    chunks = 32
     count = two // 4
+    chunks = math.gcd(count, planes)
     in_vmem = pl.BlockSpec(memory_space=pltpu.VMEM)
-    field = pl.pallas_call(
-        functools.partial(middle_kernel, chunks),
-        in_specs=[anywhere, anywhere, in_vmem, in_vmem],
-        out_specs=anywhere,
-        out_shape=jax.ShapeDtypeStruct((slots, 2, two // 2, planes, width), f32),
+    field, weights = pl.pallas_call(
+        functools.partial(middle_kernel, chunks, scale),
+        in_specs=[pl.BlockSpec(memory_space=pltpu.SMEM)] + [anywhere] * 3 + [in_vmem] * 2,
+        out_specs=[anywhere, anywhere],
+        out_shape=[
+            jax.ShapeDtypeStruct((slots, 2, two // 2, planes, width), f32),
+            jax.ShapeDtypeStruct((slots, planes, lines, three), f32),
+        ],
         scratch_shapes=[
+            pltpu.VMEM((planes, lines, three), f32),
+            pltpu.VMEM((2, slots, planes // chunks, lines, three), f32),
             pltpu.VMEM((size_px, two // 2, planes, width), f32),
             pltpu.VMEM((slots, one // 2 + 16, local, width), spectra.dtype),
             pltpu.VMEM((count + 1 + local, slots, one // 2 + 8, width), f32),
@@ -686,10 +732,12 @@
             dma((slots, chunks)),
             dma,
             dma,
+            dma,
+            dma((chunks,)),
         ],
         compiler_params=params(collective_id=0, has_side_effects=True),
         name="middle",
-    )(field, spectra, left_one, left_one_back)
+    )(chosen, field, spectra, saved, left_one, left_one_back)
     field = pl.pallas_call(
         functools.partial(second_back_kernel, slots * steps),
         grid=(slots, steps),
@@ -707,22 +755,20 @@
         compiler_params=params(collective_id=2, has_side_effects=True),
         name="second_back",
     )(field, left_two_back)
-    scale = 1.0 / (one * two * three)
-    piece = 4
+    piece = 8
     return pl.pallas_call(
-        functools.partial(third_back_kernel, scale),
+        third_back_kernel,
         grid=(planes // piece,),
         in_specs=[
-            pl.BlockSpec(memory_space=pltpu.SMEM),
             pl.BlockSpec((size_py, slots, piece, lines, width), lambda i: (0, 0, i, 0, 0)),
-            pl.BlockSpec((piece, lines, three), lambda i: (i, 0, 0)),
+            pl.BlockSpec((slots, piece, lines, three), lambda i: (0, i, 0, 0)),
             whole(right_three),
         ],
         out_specs=pl.BlockSpec((piece, lines, three), lambda i: (i, 0, 0)),
         out_shape=jax.ShapeDtypeStruct((planes, lines, three), f32),
         compiler_params=params(),
         name="third_back",
-    )(chosen, field, saved, right_three)
+    )(field, weights, right_three)
 
 
 def on_device(adjoint, saved, spectra, freq_index, picked):

time: 261 us -> 258 us (0.989)
  Pallas kernels: 256 us -> 253 us
    pallas_call x2, Pallas kernels: 228 us -> 224 us  [the longest x1 215 us: kernel_path(): pl.pallas_call(functools.partial(middle_kernel, chunks, scale), in_specs=...]
where the time goes in v3:
time: 258 us; the launch traced here: 255 us
  Pallas kernels  253 us (98%)
    pallas_call x1, Pallas kernels, kernel_path(): pl.pallas_call(functools.partial(middle_kernel, chunks, scale), in_specs=...  215 us
    pallas_call x1, Pallas kernels, kernel_path(): pl.pallas_call(functools.partial(second_back_kernel, slots * steps), grid...  15.7 us
    pallas_call x1, Pallas kernels, kernel_path(): pl.pallas_call(third_back_kernel, grid=(planes // piece,), in_specs=[pl.B...  9.56 us
    pallas_call x1, Pallas kernels, kernel_path(): pl.pallas_call(functools.partial(third_kernel, steps), grid=(steps,), in_...  7.11 us
    pallas_call x1, Pallas kernels, kernel_path(): pl.pallas_call(second_kernel, grid=(planes // block,), in_specs=[pl.Block...  5.97 us

profile of v3, /device:TPU:31, one launch (start us, length us, event | category | flops | bytes accessed | tf_op | source)
XLA Modules:
  0.0 254.6 jit_solution(1977847909557657835)
XLA Ops:
  0.0 1.4 fusion.chosen_ref
  1.4 7.1 %third.1.field_ref = f32[2,32,128,128]{3,2,1,0:T(8,128)} custom-call(f32[32,128,256]{2,1,0:T(8,128)} %field_ref.1, bf16[768,256]{1,0:T(8,128)(2,1)} %constant.12.clone.table_ref), custom_call_target="tpu_custom_call" | custom-call | tf_op jit(solution)/shard_map/third/pallas_call | solution.py:682
  8.5 6.0 %second.1.field_ref = f32[2,128,32,128]{3,2,1,0:T(8,128)} custom-call(f32[2,32,128,128]{3,2,1,0:T(8,128)} %third.1.field_ref, bf16[256,768]{1,0:T(8,128)(2,1)} %constant.13.clone.table_ref), custom_call_target="tpu_custom_call" | custom-call | tf_op jit(solution)/shard_map/second/pallas_call | solution.py:692
  14.4 214.9 %middle.1 = (f32[2,2,128,32,128]{4,3,2,1,0:T(8,128)}, f32[2,32,128,256]{3,2,1,0:T(8,128)}) custom-call(s32[2]{0:T(128)} %fusion.chosen_ref, f32[2,128,32,128]{3,2,1,0:T(8,128)} %second.1.field_ref, bf16[2,256,32,256]{3,2,1,0:T(8,128)(2,1)} %spectra_ref.1, f32[32,128,256]{2,1,0:T(8,128)} %saved_ref.1, bf16[256,768]{1,0:T(8,128)(2,1)} %constant.15.clone.ahead_ref, ...), custom_call_target="tpu_custom_call" | custom-call | tf_op jit(solution)/shard_map/middle/pallas_call | solution.py:708
  229.4 15.7 %second_back.1.field_ref = f32[2,2,32,128,128]{4,3,2,1,0:T(8,128)} custom-call(f32[2,2,128,32,128]{4,3,2,1,0:T(8,128)} %get-tuple-element.7.field_ref, bf16[256,768]{1,0:T(8,128)(2,1)} %constant.14.clone.table_ref), custom_call_target="tpu_custom_call" | custom-call | tf_op jit(solution)/shard_map/second_back/pallas_call | solution.py:741
  245.1 9.6 %third_back.1 = f32[32,128,256]{2,1,0:T(8,128)} custom-call(f32[2,2,32,128,128]{4,3,2,1,0:T(8,128)} %second_back.1.field_ref, f32[2,32,128,256]{3,2,1,0:T(8,128)} %get-tuple-element.8.weight_ref, bf16[768,256]{1,0:T(8,128)(2,1)} %constant.12.clone.table_ref), custom_call_target="tpu_custom_call" | custom-call | tf_op jit(solution)/shard_map/third_back/pallas_call | solution.py:759

commit v4 on v3

--- a/solution.py
+++ b/solution.py
@@ -425,8 +425,8 @@
     pl.semaphore_wait(barrier, everyone - 1)
 
     def send_own(chunk):
+        to_mate(chunk).start()
         own_on(chunk).start()
-        to_mate(chunk).start()
 
     def convert():
         fetch.wait()
@@ -755,7 +755,7 @@
         compiler_params=params(collective_id=2, has_side_effects=True),
         name="second_back",
     )(field, left_two_back)
-    piece = 8
+    piece = 16
     return pl.pallas_call(
         third_back_kernel,
         grid=(planes // piece,),

time: 258 us -> 258 us (level)
  no operation moved by 1% of the time
where the time goes in v4:
time: 258 us; the launch traced here: 254 us
  Pallas kernels  253 us (98%)
    pallas_call x1, Pallas kernels, kernel_path(): pl.pallas_call(functools.partial(middle_kernel, chunks, scale), in_specs=...  215 us
    pallas_call x1, Pallas kernels, kernel_path(): pl.pallas_call(functools.partial(second_back_kernel, slots * steps), grid...  15.7 us
    pallas_call x1, Pallas kernels, kernel_path(): pl.pallas_call(third_back_kernel, grid=(planes // piece,), in_specs=[pl.B...  9.12 us
    pallas_call x1, Pallas kernels, kernel_path(): pl.pallas_call(functools.partial(third_kernel, steps), grid=(steps,), in_...  7.11 us
    pallas_call x1, Pallas kernels, kernel_path(): pl.pallas_call(second_kernel, grid=(planes // block,), in_specs=[pl.Block...  5.97 us

profile of v4, /device:TPU:31, one launch (start us, length us, event | category | flops | bytes accessed | tf_op | source)
XLA Modules:
  0.0 254.2 jit_solution(17448114134140347278)
XLA Ops:
  0.0 1.4 fusion.chosen_ref
  1.4 7.1 %third.1.field_ref = f32[2,32,128,128]{3,2,1,0:T(8,128)} custom-call(f32[32,128,256]{2,1,0:T(8,128)} %field_ref.1, bf16[768,256]{1,0:T(8,128)(2,1)} %constant.12.clone.table_ref), custom_call_target="tpu_custom_call" | custom-call | tf_op jit(solution)/shard_map/third/pallas_call | solution.py:682
  8.5 6.0 %second.1.field_ref = f32[2,128,32,128]{3,2,1,0:T(8,128)} custom-call(f32[2,32,128,128]{3,2,1,0:T(8,128)} %third.1.field_ref, bf16[256,768]{1,0:T(8,128)(2,1)} %constant.13.clone.table_ref), custom_call_target="tpu_custom_call" | custom-call | tf_op jit(solution)/shard_map/second/pallas_call | solution.py:692
  14.4 214.9 %middle.1 = (f32[2,2,128,32,128]{4,3,2,1,0:T(8,128)}, f32[2,32,128,256]{3,2,1,0:T(8,128)}) custom-call(s32[2]{0:T(128)} %fusion.chosen_ref, f32[2,128,32,128]{3,2,1,0:T(8,128)} %second.1.field_ref, bf16[2,256,32,256]{3,2,1,0:T(8,128)(2,1)} %spectra_ref.1, f32[32,128,256]{2,1,0:T(8,128)} %saved_ref.1, bf16[256,768]{1,0:T(8,128)(2,1)} %constant.15.clone.ahead_ref, ...), custom_call_target="tpu_custom_call" | custom-call | tf_op jit(solution)/shard_map/middle/pallas_call | solution.py:708
  229.4 15.7 %second_back.1.field_ref = f32[2,2,32,128,128]{4,3,2,1,0:T(8,128)} custom-call(f32[2,2,128,32,128]{4,3,2,1,0:T(8,128)} %get-tuple-element.7.field_ref, bf16[256,768]{1,0:T(8,128)(2,1)} %constant.14.clone.table_ref), custom_call_target="tpu_custom_call" | custom-call | tf_op jit(solution)/shard_map/second_back/pallas_call | solution.py:741
  245.1 9.1 %third_back.1 = f32[32,128,256]{2,1,0:T(8,128)} custom-call(f32[2,2,32,128,128]{4,3,2,1,0:T(8,128)} %second_back.1.field_ref, f32[2,32,128,256]{3,2,1,0:T(8,128)} %get-tuple-element.8.weight_ref, bf16[768,256]{1,0:T(8,128)(2,1)} %constant.12.clone.table_ref), custom_call_target="tpu_custom_call" | custom-call | tf_op jit(solution)/shard_map/third_back/pallas_call | solution.py:759
